TPU v7x, 512 devices: a whole 4x8x8 slice. The times are simulated.
512 devices in a mesh: dp: 32 (over x, y), expert: 16 (over z, core).
Axes of the slice: x: 4, y: 8, z: 8, core: 2. Of those that a mesh axis runs over, the one named last changes fastest.
Arguments:
- tokens: bfloat16 [8192, 2048], P('expert', 'dp'), may hold values from -6 to 6
- routes: int32 [8192, 2], P('expert'), may hold values from 0 to 15, all different within a row; in each aligned block of 512 rows (0 to 511, 512 to 1023, ...) at most 96 rows name the same one
- scores: int32 [8192, 2], P('expert'), may hold values from 1 to 1023
- gate_weight: bfloat16 [16, 2048, 8192], P('expert', None, 'dp'), may hold values from -0.125 to 0.125
- up_weight: bfloat16 [16, 2048, 8192], P('expert', None, 'dp'), may hold values from -0.125 to 0.125
- down_weight: bfloat16 [16, 8192, 2048], P('expert', 'dp'), may hold values from -0.0625 to 0.0625
Outputs:
- layer_out: bfloat16 [8192, 2048], P('expert', 'dp')
Inputs may be any that keep to these rules, and one draw needn't show every extreme that they name: `routes`: each row names 2 different experts. Within each aligned block of 512 rows no expert is named by more than 96 rows, and in every draw some expert is named by exactly 96 rows of a block.
All inputs are finite; a program needn't handle non-finite values.
Results may differ from a plain program's by a relative error of at most 0.025.
Values may be sent and summed in bfloat16 or wider, within the bound.
A program may use at most 64 MiB of HBM per device.

v0:
```python
import jax
import jax.numpy as jnp
from jax import lax
from jax.sharding import PartitionSpec as P


def shards(tokens, routes, scores, gate_weight, up_weight, down_weight):
    expert_count = lax.axis_size("expert")
    row_count = tokens.shape[0]
    local_cols = tokens.shape[1]
    capacity = 3 * row_count // expert_count
    slot_count = expert_count * capacity
    expert_ids = jnp.arange(expert_count, dtype=jnp.int32)
    onehot = (routes[:, :, None] == expert_ids[None, None, :]).astype(jnp.int32)
    named = jnp.sum(onehot, axis=1)
    earlier = jnp.cumsum(named, axis=0) - named
    slot_rank = jnp.sum(onehot * earlier[:, None, :], axis=2)
    target = routes * capacity + slot_rank
    slot_ids = jnp.arange(slot_count, dtype=jnp.int32)
    placement = jnp.any(target[None, :, :] == slot_ids[:, None, None], axis=2).astype(jnp.bfloat16)
    weight = scores.astype(jnp.float32)
    weight = weight / jnp.sum(weight, axis=1, keepdims=True)
    gate_mat = gate_weight[0]
    up_mat = up_weight[0]
    down_mat = down_weight[0]
    outgoing = jnp.dot(placement, tokens, preferred_element_type=jnp.float32).astype(jnp.bfloat16)
    arrived = lax.all_to_all(
        outgoing.reshape(expert_count, capacity, local_cols),
        "expert",
        split_axis=0,
        concat_axis=0,
        tiled=True,
    )
    arrived = arrived.reshape(slot_count, local_cols)
    piece = lax.all_gather(arrived, "dp", axis=1, tiled=True)
    gate = jnp.dot(piece, gate_mat, preferred_element_type=jnp.float32)
    upval = jnp.dot(piece, up_mat, preferred_element_type=jnp.float32)
    hidden = (jax.nn.silu(gate) * upval).astype(jnp.bfloat16)
    summed = lax.psum_scatter(
        lax.dot_general(
            down_mat, hidden, (((0,), (1,)), ((), ())), preferred_element_type=jnp.float32
        ).astype(jnp.bfloat16),
        "dp",
        scatter_dimension=0,
        tiled=True,
    ).astype(jnp.float32)
    returned = lax.all_to_all(
        summed.reshape(local_cols, expert_count, capacity).astype(jnp.bfloat16),
        "expert",
        split_axis=1,
        concat_axis=1,
        tiled=True,
    ).astype(jnp.float32)
    returned = returned.reshape(local_cols, slot_count)
    first_part = jnp.take(returned, target[:, 0], axis=1)
    second_part = jnp.take(returned, target[:, 1], axis=1)
    combined = (first_part * weight[:, 0][None, :] + second_part * weight[:, 1][None, :]).T
    return combined.astype(jnp.bfloat16)


def solution(mesh):
    return jax.shard_map(
        shards,
        mesh=mesh,
        in_specs=(
            P("expert", "dp"),
            P("expert", None),
            P("expert", None),
            P("expert", None, "dp"),
            P("expert", None, "dp"),
            P("expert", "dp", None),
        ),
        out_specs=P("expert", "dp"),
        check_vma=False,
    )
```

profile of v0, /device:TPU:1, one launch (start us, length us, event | category | flops | bytes accessed | tf_op | source)
XLA Modules:
  0.0 414.6 jit_solution(14097522096676943779)
XLA Ops:
  6.5 0.8 convert_reduce_fusion
  7.3 1.2 reduce-window.6
  8.5 0.2 slice_reduce_fusion
  8.8 0.7 select_reduce_fusion
  9.6 0.7 multiply_add_fusion
  10.3 2.0 fusion.1
  12.2 1.4 convolution_convert_fusion.1
  13.7 0.2 reshape.37
  14.0 23.3 %all_to_all.10 = bf16[16,96,64]{1,2,0:T(8,128)(2,1)S(1)} all-to-all(bf16[16,96,64]{1,2,0:T(8,128)(2,1)S(1)} %copy.37), channel_id=1, replica_groups=mesh['dp'=32,'expert'=16] {'expert'}, dimensions={0} | all-to-all | bytes 393216 | tf_op jit(solution)/shard_map/all_to_all | solution.py:27
  37.5 0.9 reshape.38
  38.5 89.9 %all-gather.2.cloned.1.call-done = bf16[1536,2048]{0,1:T(8,128)(2,1)} async-done(((bf16[1536,64]{0,1:T(8,128)(2,1)}), bf16[1536,2048]{0,1:T(8,128)(2,1)}) %all-gather.2.cloned.1.call-update) | async-done | bytes 6291472 | tf_op jit(solution)/shard_map/all_gather | solution.py:35
  128.4 6.1 %fusion.6 = f32[1536,256]{1,0:T(8,128)} fusion(bf16[1536,2048]{0,1:T(8,128)(2,1)} %all-gather.2.cloned.1.call-done, bf16[1,2048,256]{2,1,0:T(8,128)(2,1)} %param.11), kind=kOutput, calls=%fused_computation.11 | convolution fusion | flops 1610612736 | bytes 8912896 | tf_op jit(solution)/shard_map/dot_general | solution.py:36
  134.5 12.3 %fusion = bf16[2048,1536]{0,1:T(8,128)(2,1)} fusion(bf16[1536,2048]{0,1:T(8,128)(2,1)} %all-gather.2.cloned.1.call-done, f32[1536,256]{1,0:T(8,128)} %fusion.6, bf16[1,256,2048]{2,1,0:T(8,128)(2,1)S(1)} %copy-done, bf16[1,2048,256]{2,1,0:T(8,128)(2,1)S(1)} %copy-done.2), kind=kOutput, calls=%fused_computation.3 | convolution fusion | flops 3226730496 | bytes 16252928 | tf_op jit(solution)/shard_map/dot_general | solution.py:40
  146.8 8.7 %copy.42 = bf16[2048,1536]{1,0:T(8,128)(2,1)} copy(bf16[2048,1536]{0,1:T(8,128)(2,1)} %fusion) | data formatting | bytes 12582912
  155.5 0.7 copy-done.1
  156.3 222.8 %reduce-scatter.4.cloned.1.call-done = bf16[64,1536]{1,0:T(8,128)(2,1)} async-done(((bf16[2048,1536]{1,0:T(8,128)(2,1)}), bf16[64,1536]{1,0:T(8,128)(2,1)}) %reduce-scatter.4.cloned.1.call-update) | async-done | bytes 196624
  379.0 1.1 copy.43
  380.2 0.9 copy.39
  381.0 11.6 %all-to-all-start.1 = ((bf16[64,16,96]{2,0,1:T(8,128)(2,1)}), bf16[64,16,96]{2,0,1:T(8,128)(2,1)S(1)}, u32[]{:S(2)}, u32[]{:S(2)}) async-start(bf16[64,16,96]{2,0,1:T(8,128)(2,1)} %copy.39), calls=%async_computation.1 | async-start | bytes 524288 | tf_op jit(solution)/shard_map/all_to_all | solution.py:47
  392.7 11.7 %all-to-all-done.1 = bf16[64,16,96]{2,0,1:T(8,128)(2,1)S(1)} async-done(((bf16[64,16,96]{2,0,1:T(8,128)(2,1)}), bf16[64,16,96]{2,0,1:T(8,128)(2,1)S(1)}, u32[]{:S(2)}, u32[]{:S(2)}) %all-to-all-start.1) | async-done | bytes 196640 | tf_op jit(solution)/shard_map/all_to_all | solution.py:47
  404.6 1.0 gather_fusion
  405.6 1.0 gather_fusion.1
  406.6 0.3 fusion.11
  407.0 0.7 copy.41
  (25 shorter events, 0.7 us)
Async XLA Ops:
  6.5 128.0 %copy-start = (bf16[1,256,2048]{2,1,0:T(8,128)(2,1)S(1)}, bf16[1,256,2048]{2,1,0:T(8,128)(2,1)}, u32[]{:S(2)}) copy-start(bf16[1,256,2048]{2,1,0:T(8,128)(2,1)} %param.13) | copy-start | bytes 3145732
  6.5 121.9 %all-gather.2.cloned.1.call-start = ((), (), s32[]{:S(2)}) async-start(), calls=%async_computation.3 | async-start | bytes 6488064 | tf_op jit(solution)/shard_map/all_gather | solution.py:35
  38.5 96.0 %copy-start.2 = (bf16[1,2048,256]{2,1,0:T(8,128)(2,1)S(1)}, bf16[1,2048,256]{2,1,0:T(8,128)(2,1)}, u32[]{:S(2)}) copy-start(bf16[1,2048,256]{2,1,0:T(8,128)(2,1)} %param.12) | copy-start | bytes 3145732
  38.5 340.5 %reduce-scatter.4.cloned.1.call-start = ((), (), s32[]{:S(2)}) async-start(), calls=%async_computation.4 | async-start | bytes 6488064
  155.5 0.7 copy-start.1
  381.0 23.3 %all-to-all-start.1 = ((bf16[64,16,96]{2,0,1:T(8,128)(2,1)}), bf16[64,16,96]{2,0,1:T(8,128)(2,1)S(1)}, u32[]{:S(2)}, u32[]{:S(2)}) async-start(bf16[64,16,96]{2,0,1:T(8,128)(2,1)} %copy.39), calls=%async_computation.1 | async-start | bytes 524288 | tf_op jit(solution)/shard_map/all_to_all | solution.py:47
Sparse Core Ops, SparseCore 0:
  38.6 89.7 all-gather.1
  155.6 223.3 reduce-scatter.3
where the time goes:
time: 415 us
  waiting for transfers between devices  324 us (78%)
  blocking collectives  23.3 us (6%)
  matrix products  19.8 us (5%)
  local copies, waits for them, and re-layouts  16 us (4%)
  between operations  13.5 us (3%)
  starting transfers between devices  11.7 us (3%)
  other arithmetic  5.85 us (1%)
    unnamed x3, waiting for transfers between devices  223 us
    all_gather x1, waiting for transfers between devices, shards(): piece = lax.all_gather(arrived, 'dp', axis=1, tiled=True)  89.9 us
    all_to_all x1, blocking collectives, shards(): lax.all_to_all(outgoing.reshape(expert_count, capacity, local_cols), 'exp...  23.3 us
    dot_general x1, matrix products, shards(): lax.dot_general(down_mat, hidden, (((0,), (1,)), ((), ())), preferred_ele...  12.3 us
    all_to_all x1, waiting for transfers between devices, shards(): lax.all_to_all(summed.reshape(local_cols, expert_count, capacity).astype(...  11.7 us
    all_to_all x1, starting transfers between devices, shards(): lax.all_to_all(summed.reshape(local_cols, expert_count, capacity).astype(...  11.6 us
    unnamed x8, local copies, waits for them, and re-layouts  10.5 us
  transfers between devices with their start and end apart: 3, of which 3 were waited for; matrix products, arithmetic and copies ran while one was open for 0% of the time, Pallas kernels for 0%

commit v1 on v0

--- a/solution.py
+++ b/solution.py
@@ -44,12 +44,20 @@
         scatter_dimension=0,
         tiled=True,
     ).astype(jnp.float32)
-    returned = lax.all_to_all(
-        summed.reshape(local_cols, expert_count, capacity).astype(jnp.bfloat16),
-        "expert",
-        split_axis=1,
-        concat_axis=1,
-        tiled=True,
+    returned = jnp.concatenate(
+        lax.all_to_all(
+            jnp.stack(
+                jnp.split(
+                    summed.reshape(local_cols, expert_count, capacity).astype(jnp.bfloat16),
+                    lax.axis_size("expert"),
+                    axis=1,
+                )
+            ),
+            "expert",
+            0,
+            0,
+        ),
+        axis=1,
     ).astype(jnp.float32)
     returned = returned.reshape(local_cols, slot_count)
     first_part = jnp.take(returned, target[:, 0], axis=1)

time: 415 us -> 426 us (1.027)
  local copies, waits for them, and re-layouts: 16 us -> 26.4 us
    unnamed x8 -> x39, local copies, waits for them, and re-layouts: 10.5 us -> 21 us
where the time goes in v1:
time: 426 us; the launch traced here: 425 us
  waiting for transfers between devices  324 us (76%)
  local copies, waits for them, and re-layouts  26.4 us (6%)
  blocking collectives  23.3 us (5%)
  matrix products  19.9 us (5%)
  between operations  13.7 us (3%)
  starting transfers between devices  11.8 us (3%)
  other arithmetic  5.89 us (1%)
    unnamed x3, waiting for transfers between devices  223 us
    all_gather x1, waiting for transfers between devices, shards(): piece = lax.all_gather(arrived, 'dp', axis=1, tiled=True)  89.7 us
    all_to_all x1, blocking collectives, shards(): lax.all_to_all(outgoing.reshape(expert_count, capacity, local_cols), 'exp...  23.3 us
    unnamed x39, local copies, waits for them, and re-layouts  21 us
    dot_general x1, matrix products, shards(): lax.dot_general(down_mat, hidden, (((0,), (1,)), ((), ())), preferred_ele...  12.3 us
    all_to_all x1, waiting for transfers between devices, shards(): lax.all_to_all(jnp.stack(jnp.split(summed.reshape(local_cols, expert_coun...  11.7 us
    all_to_all x1, starting transfers between devices, shards(): lax.all_to_all(jnp.stack(jnp.split(summed.reshape(local_cols, expert_coun...  11.6 us
  transfers between devices with their start and end apart: 3, of which 3 were waited for; matrix products, arithmetic and copies ran while one was open for 0% of the time, Pallas kernels for 0%

profile of v1, /device:TPU:1, one launch (start us, length us, event | category | flops | bytes accessed | tf_op | source)
XLA Modules:
  0.0 425.2 jit_solution(3388124802342850777)
XLA Ops:
  6.5 0.8 convert_reduce_fusion
  7.3 1.2 reduce-window.6
  8.8 0.7 select_reduce_fusion
  9.6 0.7 multiply_add_fusion
  10.3 2.0 fusion.1
  12.2 1.4 convolution_convert_fusion.1
  14.0 23.3 %all_to_all.10 = bf16[16,96,64]{1,2,0:T(8,128)(2,1)S(1)} all-to-all(bf16[16,96,64]{1,2,0:T(8,128)(2,1)S(1)} %copy.67), channel_id=1, replica_groups=mesh['dp'=32,'expert'=16] {'expert'}, dimensions={0} | all-to-all | bytes 393216 | tf_op jit(solution)/shard_map/all_to_all | solution.py:27
  37.5 0.9 reshape.38
  38.7 89.7 %all-gather.2.cloned.1.call-done = bf16[1536,2048]{0,1:T(8,128)(2,1)} async-done(((bf16[1536,64]{0,1:T(8,128)(2,1)}), bf16[1536,2048]{0,1:T(8,128)(2,1)}) %all-gather.2.cloned.1.call-update) | async-done | bytes 6291472 | tf_op jit(solution)/shard_map/all_gather | solution.py:35
  128.4 6.1 %fusion.6 = f32[1536,256]{1,0:T(8,128)} fusion(bf16[1536,2048]{0,1:T(8,128)(2,1)} %all-gather.2.cloned.1.call-done, bf16[1,2048,256]{2,1,0:T(8,128)(2,1)} %param.11), kind=kOutput, calls=%fused_computation.11 | convolution fusion | flops 1610612736 | bytes 8912896 | tf_op jit(solution)/shard_map/dot_general | solution.py:36
  134.5 12.3 %fusion = bf16[2048,1536]{0,1:T(8,128)(2,1)} fusion(bf16[1536,2048]{0,1:T(8,128)(2,1)} %all-gather.2.cloned.1.call-done, f32[1536,256]{1,0:T(8,128)} %fusion.6, bf16[1,256,2048]{2,1,0:T(8,128)(2,1)S(1)} %copy-done, bf16[1,2048,256]{2,1,0:T(8,128)(2,1)S(1)} %copy-done.2), kind=kOutput, calls=%fused_computation.3 | convolution fusion | flops 3226730496 | bytes 16252928 | tf_op jit(solution)/shard_map/dot_general | solution.py:40
  146.8 8.7 %copy.87 = bf16[2048,1536]{1,0:T(8,128)(2,1)} copy(bf16[2048,1536]{0,1:T(8,128)(2,1)} %fusion) | data formatting | bytes 12582912
  155.5 0.7 copy-done.1
  156.2 222.9 %reduce-scatter.4.cloned.1.call-done = bf16[64,1536]{1,0:T(8,128)(2,1)} async-done(((bf16[2048,1536]{1,0:T(8,128)(2,1)}), bf16[64,1536]{1,0:T(8,128)(2,1)}) %reduce-scatter.4.cloned.1.call-update) | async-done | bytes 196624
  379.1 1.2 copy.88
  380.4 0.6 constant_dynamic-update-slice_fusion.15
  382.6 0.6 constant_dynamic-update-slice_fusion.14
  388.6 0.6 constant_dynamic-update-slice_fusion.4
  390.4 0.6 constant_dynamic-update-slice_fusion.1
  391.6 11.6 %all-to-all-start.1 = ((bf16[16,64,1,96]{3,1,2,0:T(8,128)(2,1)}), bf16[16,64,1,96]{3,1,2,0:T(8,128)(2,1)S(1)}, u32[]{:S(2)}, u32[]{:S(2)}) async-start(bf16[16,64,1,96]{3,1,2,0:T(8,128)(2,1)} %constant_dynamic-update-slice_fusion), calls=%async_computation.1 | async-start | bytes 524288 | tf_op jit(solution)/shard_map/all_to_all | solution.py:48
  403.2 11.7 %all-to-all-done.1 = bf16[16,64,1,96]{3,1,2,0:T(8,128)(2,1)S(1)} async-done(((bf16[16,64,1,96]{3,1,2,0:T(8,128)(2,1)}), bf16[16,64,1,96]{3,1,2,0:T(8,128)(2,1)S(1)}, u32[]{:S(2)}, u32[]{:S(2)}) %all-to-all-start.1) | async-done | bytes 196640 | tf_op jit(solution)/shard_map/all_to_all | solution.py:48
  415.2 1.0 gather_fusion
  416.3 1.0 gather_fusion.1
  417.6 0.7 copy.86
  (57 shorter events, 10.5 us)
Async XLA Ops:
  6.5 128.0 %copy-start = (bf16[1,256,2048]{2,1,0:T(8,128)(2,1)S(1)}, bf16[1,256,2048]{2,1,0:T(8,128)(2,1)}, u32[]{:S(2)}) copy-start(bf16[1,256,2048]{2,1,0:T(8,128)(2,1)} %param.13) | copy-start | bytes 3145732
  6.5 121.9 %all-gather.2.cloned.1.call-start = ((), (), s32[]{:S(2)}) async-start(), calls=%async_computation.3 | async-start | bytes 6488064 | tf_op jit(solution)/shard_map/all_gather | solution.py:35
  38.5 96.0 %copy-start.2 = (bf16[1,2048,256]{2,1,0:T(8,128)(2,1)S(1)}, bf16[1,2048,256]{2,1,0:T(8,128)(2,1)}, u32[]{:S(2)}) copy-start(bf16[1,2048,256]{2,1,0:T(8,128)(2,1)} %param.12) | copy-start | bytes 3145732
  38.5 340.6 %reduce-scatter.4.cloned.1.call-start = ((), (), s32[]{:S(2)}) async-start(), calls=%async_computation.4 | async-start | bytes 6488064
  155.5 0.7 copy-start.1
  391.6 23.3 %all-to-all-start.1 = ((bf16[16,64,1,96]{3,1,2,0:T(8,128)(2,1)}), bf16[16,64,1,96]{3,1,2,0:T(8,128)(2,1)S(1)}, u32[]{:S(2)}, u32[]{:S(2)}) async-start(bf16[16,64,1,96]{3,1,2,0:T(8,128)(2,1)} %constant_dynamic-update-slice_fusion), calls=%async_computation.1 | async-start | bytes 524288 | tf_op jit(solution)/shard_map/all_to_all | solution.py:48
Sparse Core Ops, SparseCore 0:
  38.6 89.7 all-gather.1
  155.6 223.4 reduce-scatter.3
